TPU v7x, 32 devices: a whole 2x2x4 slice. The times are simulated.
32 devices in a mesh: dp: 8 (over z, y), mp: 4 (over x, core).
Axes of the slice: x: 2, y: 2, z: 4, core: 2. Of those that a mesh axis runs over, the one named last changes fastest.
Arguments:
- tokens: bfloat16 [16384, 1024], P(('dp', 'mp')), may hold values from -6 to 6
- segment_ids: int32 [16384], P(('dp', 'mp')), may hold values from 0 to 63, never falling along the last dimension, each value on 1 to 512 neighbouring positions
- w_qkv: bfloat16 [3, 1024, 1024], P(None, None, 'mp'), may hold values from -0.1875 to 0.1875
- b_qv: bfloat16 [2, 1024], P(None, 'mp'), may hold values from -1.75 to 1.75
- w_out: bfloat16 [1024, 1024], P('mp'), may hold values from -2 to 2
- b_out: bfloat16 [1024], replicated, may hold values from -1.75 to 1.75
- w_up: bfloat16 [1024, 4096], P(None, 'mp'), may hold values from -0.1875 to 0.1875
- b_up: bfloat16 [4096], P('mp'), may hold values from -1.75 to 1.75
- w_down: bfloat16 [4096, 1024], P('mp'), may hold values from -0.125 to 0.125
- b_down: bfloat16 [1024], replicated, may hold values from -1.75 to 1.75
- ln_gain: float32 [2, 1024], replicated, may hold values from 0.5 to 1.5
- ln_bias: float32 [2, 1024], replicated, may hold values from -1.75 to 1.75
- out_grad: bfloat16 [16384, 1024], P(('dp', 'mp')), may hold values from -6 to 6
Outputs:
- block_out: bfloat16 [16384, 1024], P(('dp', 'mp'))
- grad_in: float32 [16384, 1024], P(('dp', 'mp'))
- grad_qkv: float32 [3, 1024, 1024], P(None, None, 'mp')
- grad_bqv: float32 [2, 1024], P(None, 'mp')
- grad_wout: float32 [1024, 1024], P('mp')
- grad_bout: float32 [1024], replicated
- grad_up: float32 [1024, 4096], P(None, 'mp')
- grad_bup: float32 [4096], P('mp')
- grad_down: float32 [4096, 1024], P('mp')
- grad_bdown: float32 [1024], replicated
- grad_gain: float32 [2, 1024], replicated
- grad_shift: float32 [2, 1024], replicated
Inputs may be any that keep to these rules, and one draw needn't show every extreme that they name: `segment_ids`: along all frames in order, segment numbers never fall; each segment covers 1 to 512 frames and one covers exactly 512; attention never crosses a row of 1024 frames.
All inputs are finite; a program needn't handle non-finite values.
Results may differ from a plain program's by a relative error of at most 0.02.
Values may be sent and summed in bfloat16 or wider, within the bound.
No kernel may reach another device: no remote copies, remote signals or barrier semaphores. Data moves between devices by JAX's collectives and lax.ppermute only.
A program may use at most 192 MiB of HBM per device.

v0:
```python
import jax
import jax.numpy as jnp
from jax import lax
from jax.sharding import PartitionSpec as P

HD = 64
LEN = 1024
QBLK = 512
EPS = 1e-05


def norm_rows(values, gain, shift):
    center = values - jnp.mean(values, axis=-1, keepdims=True)
    spread = jnp.mean(center * center, axis=-1, keepdims=True)
    return center * lax.rsqrt(spread + EPS) * gain + shift


def split_heads(flat, rows):
    return flat.reshape(rows, LEN, flat.shape[1] // HD, HD)


def block_scores(query, keys, seg_q, seg_k, offset):
    scores = jnp.einsum(
        "rqhd,rkhd->rhqk", query, keys, preferred_element_type=jnp.float32
    ) * HD ** (-0.5)
    q_pos = offset + jnp.arange(query.shape[1], dtype=jnp.int32)
    k_pos = jnp.arange(keys.shape[1], dtype=jnp.int32)
    allowed = (seg_q[:, :, None] == seg_k[:, None, :]) & (
        k_pos[None, None, :] <= q_pos[None, :, None]
    )
    return jnp.where(allowed[:, None], scores, -1e30)


def attention_forward(query, keys, values, seg_all):
    rows = query.shape[0] // LEN
    q4 = split_heads(query, rows)
    k4 = split_heads(keys, rows)
    v4 = split_heads(values, rows)
    seg2 = seg_all.reshape(rows, LEN)
    outputs = []
    totals = []
    for block in range(LEN // QBLK):
        first = block * QBLK
        end = first + QBLK
        scores = block_scores(
            q4[:, first:end], k4[:, :end], seg2[:, first:end], seg2[:, :end], first
        )
        top = jnp.max(scores, axis=-1, keepdims=True)
        expd = jnp.exp(scores - top)
        summed = jnp.sum(expd, axis=-1, keepdims=True)
        weights = (expd / summed).astype(jnp.bfloat16)
        outputs.append(
            jnp.einsum("rhqk,rkhd->rqhd", weights, v4[:, :end], preferred_element_type=jnp.float32)
        )
        totals.append(top + jnp.log(summed))
    attended = jnp.concatenate(outputs, axis=1).reshape(query.shape).astype(jnp.bfloat16)
    return (attended, totals)


def attention_backward(query, keys, values, seg_all, totals, grad_att):
    rows = query.shape[0] // LEN
    q4 = split_heads(query, rows)
    k4 = split_heads(keys, rows)
    v4 = split_heads(values, rows)
    g4 = split_heads(grad_att, rows)
    seg2 = seg_all.reshape(rows, LEN)
    scale = HD ** (-0.5)
    grad_k = jnp.zeros(k4.shape, jnp.float32)
    grad_v = jnp.zeros(v4.shape, jnp.float32)
    grad_q_parts = []
    for block in range(LEN // QBLK):
        first = block * QBLK
        end = first + QBLK
        scores = block_scores(
            q4[:, first:end], k4[:, :end], seg2[:, first:end], seg2[:, :end], first
        )
        probs = jnp.exp(scores - totals[block])
        weights = probs.astype(jnp.bfloat16)
        grad_w = jnp.einsum(
            "rqhd,rkhd->rhqk", g4[:, first:end], v4[:, :end], preferred_element_type=jnp.float32
        )
        delta = jnp.sum(probs * grad_w, axis=-1, keepdims=True)
        grad_s = (probs * (grad_w - delta)).astype(jnp.bfloat16)
        grad_q_parts.append(
            jnp.einsum("rhqk,rkhd->rqhd", grad_s, k4[:, :end], preferred_element_type=jnp.float32)
            * scale
        )
        padding = ((0, 0), (0, LEN - end), (0, 0), (0, 0))
        grad_k = grad_k + jnp.pad(
            jnp.einsum(
                "rhqk,rqhd->rkhd", grad_s, q4[:, first:end], preferred_element_type=jnp.float32
            )
            * scale,
            padding,
        )
        grad_v = grad_v + jnp.pad(
            jnp.einsum(
                "rhqk,rqhd->rkhd", weights, g4[:, first:end], preferred_element_type=jnp.float32
            ),
            padding,
        )
    shape = query.shape
    grad_q = jnp.concatenate(grad_q_parts, axis=1).reshape(shape).astype(jnp.bfloat16)
    return (
        grad_q,
        grad_k.reshape(shape).astype(jnp.bfloat16),
        grad_v.reshape(shape).astype(jnp.bfloat16),
    )


def shards(
    tokens,
    segment_ids,
    w_qkv,
    b_qv,
    w_out,
    b_out,
    w_up,
    b_up,
    w_down,
    b_down,
    ln_gain,
    ln_bias,
    out_grad,
):
    resid = tokens.astype(jnp.float32)
    qv_bias = b_qv.astype(jnp.float32)
    up_bias = b_up.astype(jnp.float32)
    local_rows = tokens.shape[0]
    normed, first_back = jax.vjp(norm_rows, resid, ln_gain[0], ln_bias[0])
    lowered = normed.astype(jnp.bfloat16)
    joined, seg_all = (
        lax.all_gather(lowered, "mp", axis=0, tiled=True),
        lax.all_gather(segment_ids, "mp", axis=0, tiled=True),
    )
    query = (jnp.dot(joined, w_qkv[0], preferred_element_type=jnp.float32) + qv_bias[0]).astype(
        jnp.bfloat16
    )
    keys = jnp.dot(joined, w_qkv[1], preferred_element_type=jnp.float32).astype(jnp.bfloat16)
    values = (jnp.dot(joined, w_qkv[2], preferred_element_type=jnp.float32) + qv_bias[1]).astype(
        jnp.bfloat16
    )
    query, keys, values = (query, keys, values)
    attended, totals = attention_forward(query, keys, values, seg_all)
    attn_sum = lax.psum_scatter(
        jnp.dot(attended, w_out, preferred_element_type=jnp.float32).astype(jnp.bfloat16),
        "mp",
        scatter_dimension=0,
        tiled=True,
    ).astype(jnp.float32)
    mixed = resid + attn_sum + b_out.astype(jnp.float32)
    normed2, second_back = jax.vjp(norm_rows, mixed, ln_gain[1], ln_bias[1])
    lowered2 = normed2.astype(jnp.bfloat16)
    joined2 = lax.all_gather(lowered2, "mp", axis=0, tiled=True)
    pre_act = jnp.dot(joined2, w_up, preferred_element_type=jnp.float32) + up_bias
    pre_act, activ = (pre_act, jax.nn.gelu(pre_act, approximate=False).astype(jnp.bfloat16))
    block_out = (
        mixed
        + lax.psum_scatter(
            jnp.dot(activ, w_down, preferred_element_type=jnp.float32).astype(jnp.bfloat16),
            "mp",
            scatter_dimension=0,
            tiled=True,
        ).astype(jnp.float32)
        + b_down.astype(jnp.float32)
    ).astype(jnp.bfloat16)
    grad_y = out_grad.astype(jnp.float32)
    grad_z = lax.all_gather(out_grad, "mp", axis=0, tiled=True)
    grad_down = jnp.einsum("tf,td->fd", activ, grad_z, preferred_element_type=jnp.float32)
    grad_bdown = jnp.sum(grad_z, axis=0, dtype=jnp.float32)
    grad_act = jnp.einsum("td,fd->tf", grad_z, w_down, preferred_element_type=jnp.float32)
    gelu_back = jax.vjp(lambda value: jax.nn.gelu(value, approximate=False), pre_act)[1]
    grad_pre = gelu_back(grad_act)[0].astype(jnp.bfloat16)
    grad_up = jnp.einsum("td,tf->df", joined2, grad_pre, preferred_element_type=jnp.float32)
    grad_bup = jnp.sum(grad_pre, axis=0, dtype=jnp.float32)
    grad_n2 = lax.psum_scatter(
        jnp.einsum("tf,df->td", grad_pre, w_up, preferred_element_type=jnp.float32).astype(
            jnp.bfloat16
        ),
        "mp",
        scatter_dimension=0,
        tiled=True,
    ).astype(jnp.float32)
    grad_h, grad_g2, grad_s2 = second_back(grad_n2)
    grad_h = grad_h + grad_y
    grad_branch = lax.all_gather(grad_h.astype(jnp.bfloat16), "mp", axis=0, tiled=True)
    grad_wout = jnp.einsum("tc,td->cd", attended, grad_branch, preferred_element_type=jnp.float32)
    grad_bout = jnp.sum(grad_branch, axis=0, dtype=jnp.float32)
    grad_att = jnp.einsum(
        "td,cd->tc", grad_branch, w_out, preferred_element_type=jnp.float32
    ).astype(jnp.bfloat16)
    grad_q, grad_k, grad_v = attention_backward(query, keys, values, seg_all, totals, grad_att)
    grad_qkv = jnp.stack(
        [
            jnp.einsum("td,tc->dc", joined, piece, preferred_element_type=jnp.float32)
            for piece in (grad_q, grad_k, grad_v)
        ]
    )
    grad_bqv = jnp.stack(
        [jnp.sum(grad_q, axis=0, dtype=jnp.float32), jnp.sum(grad_v, axis=0, dtype=jnp.float32)]
    )
    summed = jnp.zeros((local_rows * lax.axis_size("mp"), w_qkv.shape[1]), jnp.float32)
    for index, piece in enumerate((grad_q, grad_k, grad_v)):
        summed = summed + jnp.einsum(
            "tc,dc->td", piece, w_qkv[index], preferred_element_type=jnp.float32
        )
    grad_n1 = lax.psum_scatter(
        summed.astype(jnp.bfloat16), "mp", scatter_dimension=0, tiled=True
    ).astype(jnp.float32)
    grad_x, grad_g1, grad_s1 = first_back(grad_n1)
    grad_in = grad_x + grad_h
    weight_totals = (
        lax.psum(grad_qkv.astype(jnp.bfloat16), "dp").astype(jnp.float32),
        lax.psum(grad_bqv.astype(jnp.bfloat16), "dp").astype(jnp.float32),
        lax.psum(grad_wout.astype(jnp.bfloat16), "dp").astype(jnp.float32),
        lax.psum(grad_bout.astype(jnp.bfloat16), "dp").astype(jnp.float32),
        lax.psum(grad_up.astype(jnp.bfloat16), "dp").astype(jnp.float32),
        lax.psum(grad_bup.astype(jnp.bfloat16), "dp").astype(jnp.float32),
        lax.psum(grad_down.astype(jnp.bfloat16), "dp").astype(jnp.float32),
        lax.psum(grad_bdown.astype(jnp.bfloat16), "dp").astype(jnp.float32),
    )
    norm_totals = lax.psum(
        (jnp.stack([grad_g1, grad_g2]), jnp.stack([grad_s1, grad_s2])), ("dp", "mp")
    )
    return (block_out, grad_in) + tuple(weight_totals) + tuple(norm_totals)


def solution(mesh):
    in_specs = (
        P(("dp", "mp"), None),
        P(("dp", "mp")),
        P(None, None, "mp"),
        P(None, "mp"),
        P("mp", None),
        P(),
        P(None, "mp"),
        P("mp"),
        P("mp", None),
        P(),
        P(),
        P(),
        P(("dp", "mp"), None),
    )
    out_specs = (
        P(("dp", "mp"), None),
        P(("dp", "mp"), None),
        P(None, None, "mp"),
        P(None, "mp"),
        P("mp", None),
        P(),
        P(None, "mp"),
        P("mp"),
        P("mp", None),
        P(),
        P(),
        P(),
    )
    return jax.shard_map(shards, mesh=mesh, in_specs=in_specs, out_specs=out_specs, check_vma=False)
```

profile of v0, /device:TPU:0, one launch (start us, length us, event | category | flops | bytes accessed | tf_op | source)
XLA Modules:
  0.0 795.8 jit_solution(3557118762227939732)
XLA Ops:
  15.4 6.2 all-gather
  25.2 27.5 %all-gather.6.cloned.1.call-done = bf16[2048,1024]{1,0:T(8,128)(2,1)} async-done(((bf16[512,1024]{1,0:T(8,128)(2,1)}), bf16[2048,1024]{1,0:T(8,128)(2,1)}) %all-gather.6.cloned.1.call-update) | async-done | bytes 4194320 | tf_op jit(solution)/shard_map/all_gather | solution.py:133
  110.7 44.1 %reduce-scatter.5.cloned.1.call-done = bf16[512,1024]{1,0:T(8,128)(2,1)} async-done(((bf16[2048,1024]{1,0:T(8,128)(2,1)}), bf16[512,1024]{1,0:T(8,128)(2,1)}) %reduce-scatter.5.cloned.1.call-update) | async-done | bytes 1048592 | tf_op jit(solution)/shard_map/reduce_scatter | solution.py:145
  160.6 34.0 %all-gather.8.cloned.1.call-done = bf16[2048,1024]{1,0:T(8,128)(2,1)} async-done(((bf16[512,1024]{1,0:T(8,128)(2,1)}), bf16[2048,1024]{1,0:T(8,128)(2,1)}) %all-gather.8.cloned.1.call-update) | async-done | bytes 4194320 | tf_op jit(solution)/shard_map/all_gather | solution.py:154
  194.6 11.3 %fusion.91 = f32[2048,1024]{1,0:T(8,128)} fusion(bf16[2048,1024]{1,0:T(8,128)(2,1)} %all-gather.8.cloned.1.call-done, bf16[1024,1024]{1,0:T(8,128)(2,1)} %param.19), kind=kOutput, calls=%fused_computation.163 | convolution fusion | flops 4294967296 | bytes 14680064 | tf_op jit(solution)/shard_map/dot_general | solution.py:155
  205.9 24.6 %all-gather.10.cloned.1.call-done = bf16[2048,1024]{1,0:T(8,128)(2,1)} async-done(((bf16[512,1024]{1,0:T(8,128)(2,1)}), bf16[2048,1024]{1,0:T(8,128)(2,1)}) %all-gather.10.cloned.1.call-update) | async-done | bytes 4194320 | tf_op jit(solution)/shard_map/all_gather | solution.py:168
  230.5 27.5 %fusion.78 = (bf16[1024]{0:T(1024)(128)(2,1)S(1)}, bf16[2048,1024]{1,0:T(8,128)(2,1)S(1)}, f32[2048,1024]{1,0:T(8,128)}) fusion(f32[2048,1024]{1,0:T(8,128)} %fusion.91, f32[1024]{0:T(1024)S(1)} %convert_element_type.188, bf16[2048,1024]{1,0:T(8,128)(2,1)} %all-gather.10.cloned.1.call-done, bf16[1024,1024]{1,0:T(8,128)(2,1)S(1)} %copy-done), kind=kOutput, calls=%fused_computation.151 | convolution fusion | flops 4450155520 | bytes 27269120 | tf_op jit(solution)/shard_map/td,fd->tf/dot_general | solution.py:171
  260.0 6.2 convolution_convert_fusion.1
  266.3 10.4 %multiply_convert_fusion.2 = bf16[2048,1024]{1,0:T(8,128)(2,1)} fusion(f32[2048,1024]{1,0:T(8,128)} %get-tuple-element.31, f32[2048,1024]{1,0:T(8,128)} %fusion.91, f32[1024]{0:T(1024)S(1)} %convert_element_type.188), kind=kLoop, calls=%fused_computation.17 | loop fusion | flops 8388608 | bytes 20975616 | tf_op jit(solution)/shard_map/convert_element_type | solution.py:156
  276.7 8.4 %convolution_convert_fusion.2 = bf16[2048,1024]{1,0:T(8,128)(2,1)} fusion(bf16[2048,1024]{1,0:T(8,128)(2,1)} %multiply_convert_fusion.2, bf16[1024,1024]{1,0:T(8,128)(2,1)S(1)} %copy-done), kind=kOutput, calls=%fused_computation.43 | convolution fusion | flops 4297064448 | bytes 10485760 | tf_op jit(solution)/shard_map/dot_general | solution.py:160
  285.7 25.2 %reduce-scatter.9.cloned.1.call-done = bf16[512,1024]{1,0:T(8,128)(2,1)} async-done(((bf16[2048,1024]{1,0:T(8,128)(2,1)}), bf16[512,1024]{1,0:T(8,128)(2,1)}) %reduce-scatter.9.cloned.1.call-update) | async-done | bytes 1048592 | tf_op jit(solution)/shard_map/reduce_scatter | solution.py:176
  313.3 44.7 %reduce-scatter.7.cloned.1.call-done = bf16[512,1024]{1,0:T(8,128)(2,1)} async-done(((bf16[2048,1024]{1,0:T(8,128)(2,1)}), bf16[512,1024]{1,0:T(8,128)(2,1)}) %reduce-scatter.7.cloned.1.call-update) | async-done | bytes 1048592 | tf_op jit(solution)/shard_map/reduce_scatter | solution.py:159
  364.5 9.5 %convolution_convert_fusion.6 = bf16[1024,1024]{1,0:T(8,128)(2,1)} fusion(bf16[2048,1024]{1,0:T(8,128)(2,1)} %all-gather.8.cloned.1.call-done, bf16[2048,1024]{1,0:T(8,128)(2,1)} %copy-done.55), kind=kOutput, calls=%fused_computation.90 | convolution fusion | flops 4296015872 | bytes 10485760 | tf_op jit(solution)/shard_map/td,tf->df/dot_general | solution.py:174
  374.0 6.0 convolution_convert_fusion.5
  379.9 19.0 %all-gather.12.cloned.1.call-done = bf16[2048,1024]{1,0:T(8,128)(2,1)} async-done(((bf16[512,1024]{1,0:T(8,128)(2,1)}), bf16[2048,1024]{1,0:T(8,128)(2,1)}) %all-gather.12.cloned.1.call-update) | async-done | bytes 4194320 | tf_op jit(solution)/shard_map/all_gather | solution.py:186
  410.4 5.9 fusion.42
  429.7 14.7 %multiply_reduce_fusion = (f32[2,4,512]{2,1,0:T(4,128)S(1)}, f32[2,4,512,1024]{3,2,1,0:T(8,128)}) fusion(f32[2,4,512,1024]{3,2,1,0:T(8,128)} %copy-done.2, f32[2,4,512]{2,1,0:T(4,128)S(1)} %bitcast.140, bf16[2,512,4,64]{1,3,2,0:T(8,128)(2,1)} %copy.98, bf16[2,1024,4,64]{1,3,2,0:T(8,128)(2,1)S(1)} %copy-done.15), kind=kOutput, calls=%fused_computation.1 | convolution fusion | flops 549449728 | bytes 35160064 | tf_op jit(solution)/shard_map/rqhd,rkhd->rhqk/dot_general | solution.py:79
  444.4 7.8 fusion.90
  453.6 10.9 %multiply_convert_fusion = bf16[2,4,512,1024]{3,2,1,0:T(8,128)(2,1)} fusion(f32[2,4,512,1024]{3,2,1,0:T(8,128)} %get-tuple-element.54, f32[2,4,512,1024]{3,2,1,0:T(8,128)S(1)} %bitcast.125, f32[2,4,512]{2,1,0:T(4,128)S(1)} %get-tuple-element.53, f32[2,4,512]{2,1,0:T(4,128)S(1)} %bitcast.142), kind=kLoop, calls=%fused_computation | loop fusion | flops 16777216 | bytes 41975808 | tf_op jit(solution)/shard_map/convert_element_type | solution.py:83
  464.6 6.2 fusion.47
  497.5 23.2 %all-reduce.3 = (bf16[2,256]{1,0:T(2,128)(2,1)S(1)}, bf16[1024]{0:T(1024)(128)(2,1)S(1)}, bf16[1024]{0:T(1024)(128)(2,1)S(1)}, bf16[1024]{0:T(1024)(128)(2,1)S(1)}) all-reduce(bf16[2,256]{1,0:T(2,128)(2,1)S(1)} %pad_maximum_fusion.4, bf16[1024]{0:T(1024)(128)(2,1)S(1)} %reduce_sum.244, ...), channel_id=1, replica_groups=mesh['dp'=8,'mp'=4] {'dp'}, use_global_device_ids=true, to_apply=%region_21.22 | all-reduce | flops 3584 | bytes 14336 | tf_op jit(solution)/shard_map/psum | solution.py:214
  523.1 171.2 %all-reduce.7.cloned.1.call-done = (bf16[3,1024,256]{2,1,0:T(8,128)(2,1)}, bf16[256,1024]{1,0:T(8,128)(2,1)}, bf16[1024,1024]{1,0:T(8,128)(2,1)}, bf16[1024,1024]{1,0:T(8,128)(2,1)}) async-done(((bf16[3,1024,256]{2,1,0:T(8,128)(2,1)}, bf16[256,1024]{1,0:T(8,128)(2,1)}, bf16[1024,1024]{1,0:T(8,128)(2,1)}, bf16[1024,1024]{1,0:T(8,128)(2,1)}), (bf16[3,1024,256]{2,1,0:T(8,128)(2,1)}, ...) | async-done | bytes 6291472 | tf_op jit(solution)/shard_map/psum | solution.py:213
  705.4 35.1 %reduce-scatter.11.cloned.1.call-done = bf16[512,1024]{1,0:T(8,128)(2,1)} async-done(((bf16[2048,1024]{1,0:T(8,128)(2,1)}), bf16[512,1024]{1,0:T(8,128)(2,1)}) %reduce-scatter.11.cloned.1.call-update) | async-done | bytes 1048592 | tf_op jit(solution)/shard_map/reduce_scatter | solution.py:207
  745.1 39.5 %all-reduce.2 = (f32[2,1024]{1,0:T(2,128)}, f32[2,1024]{1,0:T(2,128)}) all-reduce(f32[2,1024]{1,0:T(2,128)S(1)} %get-tuple-element.59, f32[2,1024]{1,0:T(2,128)S(1)} %get-tuple-element.60), channel_id=1, replica_groups=mesh['dp'=8,'mp'=4] {'dp','mp'}, use_global_device_ids=true, to_apply=%region_33.34 | all-reduce | flops 4096 | bytes 32768 | tf_op jit(solution)/shard_map/psum | solution.py:222
  (240 shorter events, 161.8 us)
Async XLA Ops:
  7.2 223.3 %copy-start = (bf16[1024,1024]{1,0:T(8,128)(2,1)S(1)}, bf16[1024,1024]{1,0:T(8,128)(2,1)}, u32[]{:S(2)}) copy-start(bf16[1024,1024]{1,0:T(8,128)(2,1)} %param.21) | copy-start | bytes 6291460
  7.2 45.5 %all-gather.6.cloned.1.call-start = ((), (), s32[]{:S(2)}) async-start(), calls=%async_computation.4 | async-start | bytes 5242880 | tf_op jit(solution)/shard_map/all_gather | solution.py:133
  15.3 139.4 %reduce-scatter.5.cloned.1.call-start = ((), (), s32[]{:S(2)}) async-start(), calls=%async_computation.5 | async-start | bytes 5242880 | tf_op jit(solution)/shard_map/reduce_scatter | solution.py:145
  110.0 44.8 %copy-start.4 = (bf16[512,1024]{1,0:T(8,128)(2,1)S(1)}, bf16[512,1024]{1,0:T(8,128)(2,1)}, u32[]{:S(2)}) copy-start(bf16[512,1024]{1,0:T(8,128)(2,1)} %param.13) | copy-start | bytes 3145732
  110.0 84.5 %all-gather.8.cloned.1.call-start = ((), (), s32[]{:S(2)}) async-start(), calls=%async_computation.6 | async-start | bytes 5242880 | tf_op jit(solution)/shard_map/all_gather | solution.py:154
  159.9 70.5 %all-gather.10.cloned.1.call-start = ((), (), s32[]{:S(2)}) async-start(), calls=%async_computation.8 | async-start | bytes 5242880 | tf_op jit(solution)/shard_map/all_gather | solution.py:168
  160.5 150.5 %reduce-scatter.9.cloned.1.call-start = ((), (), s32[]{:S(2)}) async-start(), calls=%async_computation.9 | async-start | bytes 5242880 | tf_op jit(solution)/shard_map/reduce_scatter | solution.py:176
  230.5 29.5 %copy-start.54 = (bf16[1024,1024]{1,0:T(8,128)(2,1)S(1)}, bf16[1024,1024]{1,0:T(8,128)(2,1)}, u32[]{:S(2)}) copy-start(bf16[1024,1024]{1,0:T(8,128)(2,1)} %param.19) | copy-start | bytes 6291460
  266.2 91.7 %reduce-scatter.7.cloned.1.call-start = ((), (), s32[]{:S(2)}) async-start(), calls=%async_computation.7 | async-start | bytes 5242880 | tf_op jit(solution)/shard_map/reduce_scatter | solution.py:159
  285.1 25.9 %copy-start.7 = (bf16[512,1024]{1,0:T(8,128)(2,1)S(1)}, bf16[512,1024]{1,0:T(8,128)(2,1)}, u32[]{:S(2)}) copy-start(bf16[512,1024]{1,0:T(8,128)(2,1)} %reduce-scatter.5.cloned.1.call-done) | copy-start | bytes 3145732
  285.1 113.9 %all-gather.12.cloned.1.call-start = ((), (), s32[]{:S(2)}) async-start(), calls=%async_computation.10 | async-start | bytes 5242880 | tf_op jit(solution)/shard_map/all_gather | solution.py:186
  313.3 49.7 %copy-start.11 = (bf16[512,1024]{1,0:T(8,128)(2,1)S(1)}, bf16[512,1024]{1,0:T(8,128)(2,1)}, u32[]{:S(2)}) copy-start(bf16[512,1024]{1,0:T(8,128)(2,1)} %param.25) | copy-start | bytes 3145732
  364.3 330.0 %all-reduce.7.cloned.1.call-start = ((), (), s32[]{:S(2)}) async-start(), calls=%async_computation.12 | async-start | bytes 12582912 | tf_op jit(solution)/shard_map/psum | solution.py:213
  374.0 25.0 %copy-start.35 = (bf16[256,1024]{1,0:T(8,128)(2,1)S(1)}, bf16[256,1024]{1,0:T(8,128)(2,1)}, u32[]{:S(2)}) copy-start(bf16[256,1024]{1,0:T(8,128)(2,1)} %param.17) | copy-start | bytes 1572868
  429.6 23.9 %slice-start = ((s8[16777216]{0:T(1024)(128)(4,1)}), s8[4194304]{0:T(1024)(128)(4,1)S(1)}, s32[]{:S(2)}) async-start(s8[16777216]{0:T(1024)(128)(4,1)} %bitcast.124), calls=%async_computation.13 | async-start | bytes 8388608
  429.6 23.9 %slice-start.1 = ((s8[16777216]{0:T(1024)(128)(4,1)}), s8[4194304]{0:T(1024)(128)(4,1)S(1)}, s32[]{:S(2)}) async-start(s8[16777216]{0:T(1024)(128)(4,1)} %bitcast.124), calls=%async_computation.14 | async-start | bytes 8388608
  429.6 23.9 %slice-start.2 = ((s8[16777216]{0:T(1024)(128)(4,1)}), s8[4194304]{0:T(1024)(128)(4,1)S(1)}, s32[]{:S(2)}) async-start(s8[16777216]{0:T(1024)(128)(4,1)} %bitcast.124), calls=%async_computation.15 | async-start | bytes 8388608
  453.5 21.8 %copy-start.23 = (bf16[32,8,2,1024]{3,1,2,0:T(8,128)(2,1)}, bf16[32,8,2,1024]{3,1,2,0:T(8,128)(2,1)S(1)}, u32[]{:S(2)}) copy-start(bf16[32,8,2,1024]{3,1,2,0:T(8,128)(2,1)S(1)} %copy.102) | copy-start | bytes 3145732
  483.1 257.4 %reduce-scatter.11.cloned.1.call-start = ((), (), s32[]{:S(2)}) async-start(), calls=%async_computation.11 | async-start | bytes 5242880 | tf_op jit(solution)/shard_map/reduce_scatter | solution.py:207
  702.4 38.1 %copy-start.39 = (f32[1,1024]{1,0:T(1,128)S(1)}, f32[1,1024]{1,0:T(1,128)}, u32[]{:S(2)}) copy-start(f32[1,1024]{1,0:T(1,128)} %copy-done.38) | copy-start | bytes 12292
  702.4 38.1 %copy-start.41 = (f32[512]{0:T(512)S(1)}, f32[512]{0:T(512)}, u32[]{:S(2)}) copy-start(f32[512]{0:T(512)} %copy-done.40) | copy-start | bytes 6148
  702.4 40.0 %copy-start.47 = (f32[512]{0:T(512)S(1)}, f32[512]{0:T(512)}, u32[]{:S(2)}) copy-start(f32[512]{0:T(512)} %copy-done.46) | copy-start | bytes 6148
  702.4 40.0 %copy-start.45 = (f32[512]{0:T(512)S(1)}, f32[512]{0:T(512)}, u32[]{:S(2)}) copy-start(f32[512]{0:T(512)} %copy-done.44) | copy-start | bytes 6148
  742.5 46.6 %copy-start.1 = (bf16[1024,1024]{1,0:T(8,128)(2,1)S(1)}, bf16[1024,1024]{1,0:T(8,128)(2,1)}, u32[]{:S(2)}) copy-start(bf16[1024,1024]{1,0:T(8,128)(2,1)} %param.21) | copy-start | bytes 6291460
  (47 other events, 227.6 us)
Sparse Core Ops, SparseCore 0:
  15.5 37.1 all-gather.5
  110.2 44.5 reduce-scatter.4
  160.0 34.4 all-gather.7
  196.0 34.4 all-gather.9
  266.4 44.5 reduce-scatter.8
  313.4 44.5 reduce-scatter.6
  364.5 34.4 all-gather.11
  483.2 211.0 all-reduce.6
  696.9 43.6 reduce-scatter.10
where the time goes:
time: 801 us; the launch traced here: 796 us
  waiting for transfers between devices  426 us (53%)
  matrix products  158 us (20%)
  other arithmetic  80 us (10%)
  blocking collectives  68.8 us (9%)
  local copies, waits for them, and re-layouts  47.6 us (6%)
  between operations  14.9 us (2%)
    psum x1, waiting for transfers between devices, shards(): lax.psum(grad_qkv.astype(jnp.bfloat16), 'dp').astype(jnp.float32)  171 us
    reduce_scatter x1, waiting for transfers between devices, shards(): lax.psum_scatter(jnp.dot(activ, w_down, preferred_element_type=jnp.float3...  44.7 us
    reduce_scatter x1, waiting for transfers between devices, shards(): lax.psum_scatter(jnp.dot(attended, w_out, preferred_element_type=jnp.floa...  44.1 us
    psum x1, blocking collectives, shards(): lax.psum((jnp.stack([grad_g1, grad_g2]), jnp.stack([grad_s1, grad_s2])),...  39.5 us
    reduce_scatter x1, waiting for transfers between devices, shards(): lax.psum_scatter(summed.astype(jnp.bfloat16), 'mp', scatter_dimension=0,...  35.1 us
    all_gather x1, waiting for transfers between devices, shards(): joined2 = lax.all_gather(lowered2, 'mp', axis=0, tiled=True)  34 us
    dot_general x1, matrix products, shards(): jnp.einsum('td,fd->tf', grad_z, w_down, preferred_element_type=jnp.float32)  27.5 us
    all_gather x1, waiting for transfers between devices, shards(): lax.all_gather(lowered, 'mp', axis=0, tiled=True)  27.5 us
  transfers between devices with their start and end apart: 9, of which 9 were waited for; matrix products, arithmetic and copies ran while one was open for 10% of the time, Pallas kernels for 0%

commit v1 on v0

--- a/solution.py
+++ b/solution.py
@@ -7,6 +7,7 @@
 LEN = 1024
 QBLK = 512
 EPS = 1e-05
+_push_entries = lambda a0: jnp.sum(lax.all_gather(a0, "dp"), 0)
 
 
 def norm_rows(values, gain, shift):
@@ -210,7 +211,7 @@
     grad_x, grad_g1, grad_s1 = first_back(grad_n1)
     grad_in = grad_x + grad_h
     weight_totals = (
-        lax.psum(grad_qkv.astype(jnp.bfloat16), "dp").astype(jnp.float32),
+        _push_entries(grad_qkv.astype(jnp.bfloat16)).astype(jnp.float32),
         lax.psum(grad_bqv.astype(jnp.bfloat16), "dp").astype(jnp.float32),
         lax.psum(grad_wout.astype(jnp.bfloat16), "dp").astype(jnp.float32),
         lax.psum(grad_bout.astype(jnp.bfloat16), "dp").astype(jnp.float32),

time: 801 us -> 878 us (1.096)
  waiting for transfers between devices: 426 us -> 486 us
  other arithmetic: 80 us -> 93.2 us
    all_gather x0 -> x1, waiting for transfers between devices: none -> 127 us  [_push_entries = lambda a0: jnp.sum(lax.all_gather(a0, 'dp'), 0)]
    psum x1, waiting for transfers between devices: 171 us -> 103 us  [shards(): lax.psum(grad_wout.astype(jnp.bfloat16), 'dp').astype(jnp.float32)]
    unnamed x132 -> x116, local copies, waits for them, and re-layouts: 20.4 us -> 22.7 us
  transfers between devices with their start and end apart: 9 -> 10, of which waited for: 9 -> 10; matrix products, arithmetic and copies ran while one was open for 10% -> 13% of each run, Pallas kernels for 0% -> 0%
where the time goes in v1:
time: 878 us; the launch traced here: 873 us
  waiting for transfers between devices  486 us (55%)
  matrix products  155 us (18%)
  other arithmetic  93.2 us (11%)
  blocking collectives  73 us (8%)
  local copies, waits for them, and re-layouts  49.9 us (6%)
  between operations  15.2 us (2%)
    all_gather x1, waiting for transfers between devices, _push_entries = lambda a0: jnp.sum(lax.all_gather(a0, 'dp'), 0)  127 us
    psum x1, waiting for transfers between devices, shards(): lax.psum(grad_wout.astype(jnp.bfloat16), 'dp').astype(jnp.float32)  103 us
    reduce_scatter x1, waiting for transfers between devices, shards(): lax.psum_scatter(jnp.dot(activ, w_down, preferred_element_type=jnp.float3...  44.7 us
    psum x1, blocking collectives, shards(): lax.psum((jnp.stack([grad_g1, grad_g2]), jnp.stack([grad_s1, grad_s2])),...  44.4 us
    reduce_scatter x1, waiting for transfers between devices, shards(): lax.psum_scatter(jnp.dot(attended, w_out, preferred_element_type=jnp.floa...  44.1 us
    reduce_scatter x1, waiting for transfers between devices, shards(): lax.psum_scatter(summed.astype(jnp.bfloat16), 'mp', scatter_dimension=0,...  37.1 us
    all_gather x1, waiting for transfers between devices, shards(): joined2 = lax.all_gather(lowered2, 'mp', axis=0, tiled=True)  34 us
    all_gather x1, waiting for transfers between devices, shards(): lax.all_gather(lowered, 'mp', axis=0, tiled=True)  27.5 us
  transfers between devices with their start and end apart: 10, of which 10 were waited for; matrix products, arithmetic and copies ran while one was open for 13% of the time, Pallas kernels for 0%

profile of v1, /device:TPU:0, one launch (start us, length us, event | category | flops | bytes accessed | tf_op | source)
XLA Modules:
  0.0 873.0 jit_solution(8544774642151112982)
XLA Ops:
  15.4 6.2 all-gather
  25.2 27.5 %all-gather.7.cloned.1.call-done = bf16[2048,1024]{1,0:T(8,128)(2,1)} async-done(((bf16[512,1024]{1,0:T(8,128)(2,1)}), bf16[2048,1024]{1,0:T(8,128)(2,1)}) %all-gather.7.cloned.1.call-update) | async-done | bytes 4194320 | tf_op jit(solution)/shard_map/all_gather | solution.py:134
  110.7 44.1 %reduce-scatter.5.cloned.1.call-done = bf16[512,1024]{1,0:T(8,128)(2,1)} async-done(((bf16[2048,1024]{1,0:T(8,128)(2,1)}), bf16[512,1024]{1,0:T(8,128)(2,1)}) %reduce-scatter.5.cloned.1.call-update) | async-done | bytes 1048592 | tf_op jit(solution)/shard_map/reduce_scatter | solution.py:146
  160.6 34.0 %all-gather.9.cloned.1.call-done = bf16[2048,1024]{1,0:T(8,128)(2,1)} async-done(((bf16[512,1024]{1,0:T(8,128)(2,1)}), bf16[2048,1024]{1,0:T(8,128)(2,1)}) %all-gather.9.cloned.1.call-update) | async-done | bytes 4194320 | tf_op jit(solution)/shard_map/all_gather | solution.py:155
  194.6 11.3 %fusion.91 = f32[2048,1024]{1,0:T(8,128)} fusion(bf16[2048,1024]{1,0:T(8,128)(2,1)} %all-gather.9.cloned.1.call-done, bf16[1024,1024]{1,0:T(8,128)(2,1)} %param.19), kind=kOutput, calls=%fused_computation.163 | convolution fusion | flops 4294967296 | bytes 14680064 | tf_op jit(solution)/shard_map/dot_general | solution.py:156
  205.9 24.6 %all-gather.11.cloned.1.call-done = bf16[2048,1024]{1,0:T(8,128)(2,1)} async-done(((bf16[512,1024]{1,0:T(8,128)(2,1)}), bf16[2048,1024]{1,0:T(8,128)(2,1)}) %all-gather.11.cloned.1.call-update) | async-done | bytes 4194320 | tf_op jit(solution)/shard_map/all_gather | solution.py:169
  230.5 27.4 %fusion.78 = (bf16[1024]{0:T(1024)(128)(2,1)S(1)}, bf16[2048,1024]{1,0:T(8,128)(2,1)S(1)}, f32[2048,1024]{1,0:T(8,128)}) fusion(f32[2048,1024]{1,0:T(8,128)} %fusion.91, f32[1024]{0:T(1024)S(1)} %convert_element_type.197, bf16[2048,1024]{1,0:T(8,128)(2,1)} %all-gather.11.cloned.1.call-done, bf16[1024,1024]{1,0:T(8,128)(2,1)S(1)} %copy-done), kind=kOutput, calls=%fused_computation.151 | convolution fusion | flops 4450155520 | bytes 27269120 | tf_op jit(solution)/shard_map/td,fd->tf/dot_general | solution.py:172
  259.8 6.2 convolution_convert_fusion.1
  266.1 10.4 %multiply_convert_fusion.2 = bf16[2048,1024]{1,0:T(8,128)(2,1)} fusion(f32[2048,1024]{1,0:T(8,128)} %get-tuple-element.30, f32[2048,1024]{1,0:T(8,128)} %fusion.91, f32[1024]{0:T(1024)S(1)} %convert_element_type.197), kind=kLoop, calls=%fused_computation.17 | loop fusion | flops 8388608 | bytes 20975616 | tf_op jit(solution)/shard_map/convert_element_type | solution.py:157
  276.5 8.4 convolution_convert_fusion.2
  285.6 25.2 %reduce-scatter.9.cloned.1.call-done = bf16[512,1024]{1,0:T(8,128)(2,1)} async-done(((bf16[2048,1024]{1,0:T(8,128)(2,1)}), bf16[512,1024]{1,0:T(8,128)(2,1)}) %reduce-scatter.9.cloned.1.call-update) | async-done | bytes 1048592 | tf_op jit(solution)/shard_map/reduce_scatter | solution.py:177
  313.1 44.7 %reduce-scatter.7.cloned.1.call-done = bf16[512,1024]{1,0:T(8,128)(2,1)} async-done(((bf16[2048,1024]{1,0:T(8,128)(2,1)}), bf16[512,1024]{1,0:T(8,128)(2,1)}) %reduce-scatter.7.cloned.1.call-update) | async-done | bytes 1048592 | tf_op jit(solution)/shard_map/reduce_scatter | solution.py:160
  364.3 9.5 %convolution_convert_fusion.6 = bf16[1024,1024]{1,0:T(8,128)(2,1)} fusion(bf16[2048,1024]{1,0:T(8,128)(2,1)} %all-gather.9.cloned.1.call-done, bf16[2048,1024]{1,0:T(8,128)(2,1)} %copy-done.51), kind=kOutput, calls=%fused_computation.90 | convolution fusion | flops 4296015872 | bytes 10485760 | tf_op jit(solution)/shard_map/td,tf->df/dot_general | solution.py:175
  379.8 19.0 %all-gather.13.cloned.1.call-done = bf16[2048,1024]{1,0:T(8,128)(2,1)} async-done(((bf16[512,1024]{1,0:T(8,128)(2,1)}), bf16[2048,1024]{1,0:T(8,128)(2,1)}) %all-gather.13.cloned.1.call-update) | async-done | bytes 4194320 | tf_op jit(solution)/shard_map/all_gather | solution.py:187
  416.0 6.3 multiply_reduce_fusion.1
  423.9 13.3 %multiply_reduce_fusion = (f32[2,4,512]{2,1,0:T(4,128)S(1)}, f32[2,4,512,1024]{3,2,1,0:T(8,128)}) fusion(f32[2,4,512,1024]{3,2,1,0:T(8,128)} %copy-done.2, f32[2,4,512]{2,1,0:T(4,128)S(1)} %bitcast.138, bf16[2,512,4,64]{1,3,2,0:T(8,128)(2,1)S(1)} %copy.98, bf16[2,1024,4,64]{1,3,2,0:T(8,128)(2,1)S(1)} %copy-done.17), kind=kOutput, calls=%fused_computation.1 | convolution fusion | flops 549449728 | bytes 35160064 | tf_op jit(solution)/shard_map/rqhd,rkhd->rhqk/dot_general | solution.py:80
  437.2 7.6 fusion.90
  459.0 13.3 %multiply_convert_fusion = bf16[2,4,512,1024]{3,2,1,0:T(8,128)(2,1)S(1)} fusion(f32[2,4,512,1024]{3,2,1,0:T(8,128)} %get-tuple-element.53, f32[2,4,512,1024]{3,2,1,0:T(8,128)} %copy-done.2, f32[2,4,512]{2,1,0:T(4,128)S(1)} %get-tuple-element.52, f32[2,4,512]{2,1,0:T(4,128)S(1)} %bitcast.140), kind=kLoop, calls=%fused_computation | loop fusion | flops 16777216 | bytes 41975808 | tf_op jit(solution)/shard_map/convert_element_type | solution.py:84
  501.5 22.5 %all-reduce.3 = (bf16[2,256]{1,0:T(2,128)(2,1)S(1)}, bf16[1024]{0:T(1024)(128)(2,1)S(1)}, bf16[1024]{0:T(1024)(128)(2,1)S(1)}, bf16[1024]{0:T(1024)(128)(2,1)S(1)}) all-reduce(bf16[2,256]{1,0:T(2,128)(2,1)S(1)} %pad_maximum_fusion.4, bf16[1024]{0:T(1024)(128)(2,1)S(1)} %reduce_sum.257, ...), channel_id=1, replica_groups=mesh['dp'=8,'mp'=4] {'dp'}, use_global_device_ids=true, to_apply=%region_21.22 | all-reduce | flops 3584 | bytes 14336 | tf_op jit(solution)/shard_map/psum | solution.py:215
  526.4 102.9 %all-reduce.7.cloned.1.call-done = (bf16[256,1024]{1,0:T(8,128)(2,1)}, bf16[1024,1024]{1,0:T(8,128)(2,1)}, bf16[1024,1024]{1,0:T(8,128)(2,1)}) async-done(((bf16[256,1024]{1,0:T(8,128)(2,1)}, bf16[1024,1024]{1,0:T(8,128)(2,1)}, bf16[1024,1024]{1,0:T(8,128)(2,1)}), (bf16[256,1024]{1,0:T(8,128)(2,1)}, bf16[1024,1024]{1,0:T(8,128)(2,1)}, bf16[1024,1024]{1,0:T(8,128)(2,1)})) %all-reduce.7.cloned.1.call-update) | async-done | bytes 4718608 | tf_op jit(solution)/shard_map/psum | solution.py:216
  638.3 37.1 %reduce-scatter.11.cloned.1.call-done = bf16[512,1024]{1,0:T(8,128)(2,1)} async-done(((bf16[2048,1024]{1,0:T(8,128)(2,1)}), bf16[512,1024]{1,0:T(8,128)(2,1)}) %reduce-scatter.11.cloned.1.call-update) | async-done | bytes 1048592 | tf_op jit(solution)/shard_map/reduce_scatter | solution.py:208
  679.8 44.4 %all-reduce.2 = (f32[2,1024]{1,0:T(2,128)}, f32[2,1024]{1,0:T(2,128)}) all-reduce(f32[2,1024]{1,0:T(2,128)S(1)} %get-tuple-element.58, f32[2,1024]{1,0:T(2,128)S(1)} %get-tuple-element.59), channel_id=1, replica_groups=mesh['dp'=8,'mp'=4] {'dp','mp'}, use_global_device_ids=true, to_apply=%region_33.34 | all-reduce | flops 4096 | bytes 32768 | tf_op jit(solution)/shard_map/psum | solution.py:223
  728.0 126.6 %all-gather.15.cloned.1.call-done = bf16[8,3,1024,256]{3,2,1,0:T(8,128)(2,1)} async-done(((bf16[1,3,1024,256]{3,2,1,0:T(8,128)(2,1)}), bf16[8,3,1024,256]{3,2,1,0:T(8,128)(2,1)}) %all-gather.15.cloned.1.call-update) | async-done | bytes 12582928 | tf_op jit(solution)/shard_map/all_gather | solution.py:10
  854.6 8.0 reduce_sum.254
  (227 shorter events, 177.4 us)
Async XLA Ops:
  7.2 223.3 %copy-start = (bf16[1024,1024]{1,0:T(8,128)(2,1)S(1)}, bf16[1024,1024]{1,0:T(8,128)(2,1)}, u32[]{:S(2)}) copy-start(bf16[1024,1024]{1,0:T(8,128)(2,1)} %param.21) | copy-start | bytes 6291460
  7.2 14.5 %copy-start.44 = (bf16[2,256]{1,0:T(2,128)(2,1)S(1)}, bf16[2,256]{1,0:T(2,128)(2,1)}, u32[]{:S(2)}) copy-start(bf16[2,256]{1,0:T(2,128)(2,1)} %param.16) | copy-start | bytes 3076
  7.2 45.5 %all-gather.7.cloned.1.call-start = ((), (), s32[]{:S(2)}) async-start(), calls=%async_computation.4 | async-start | bytes 5242880 | tf_op jit(solution)/shard_map/all_gather | solution.py:134
  15.3 139.5 %reduce-scatter.5.cloned.1.call-start = ((), (), s32[]{:S(2)}) async-start(), calls=%async_computation.5 | async-start | bytes 5242880 | tf_op jit(solution)/shard_map/reduce_scatter | solution.py:146
  110.1 44.8 %copy-start.4 = (bf16[512,1024]{1,0:T(8,128)(2,1)S(1)}, bf16[512,1024]{1,0:T(8,128)(2,1)}, u32[]{:S(2)}) copy-start(bf16[512,1024]{1,0:T(8,128)(2,1)} %param.13) | copy-start | bytes 3145732
  110.1 84.5 %all-gather.9.cloned.1.call-start = ((), (), s32[]{:S(2)}) async-start(), calls=%async_computation.6 | async-start | bytes 5242880 | tf_op jit(solution)/shard_map/all_gather | solution.py:155
  160.0 70.5 %all-gather.11.cloned.1.call-start = ((), (), s32[]{:S(2)}) async-start(), calls=%async_computation.8 | async-start | bytes 5242880 | tf_op jit(solution)/shard_map/all_gather | solution.py:169
  160.5 150.3 %reduce-scatter.9.cloned.1.call-start = ((), (), s32[]{:S(2)}) async-start(), calls=%async_computation.9 | async-start | bytes 5242880 | tf_op jit(solution)/shard_map/reduce_scatter | solution.py:177
  230.5 29.3 %copy-start.50 = (bf16[1024,1024]{1,0:T(8,128)(2,1)S(1)}, bf16[1024,1024]{1,0:T(8,128)(2,1)}, u32[]{:S(2)}) copy-start(bf16[1024,1024]{1,0:T(8,128)(2,1)} %param.19) | copy-start | bytes 6291460
  266.1 91.7 %reduce-scatter.7.cloned.1.call-start = ((), (), s32[]{:S(2)}) async-start(), calls=%async_computation.7 | async-start | bytes 5242880 | tf_op jit(solution)/shard_map/reduce_scatter | solution.py:160
  284.9 25.9 %copy-start.8 = (bf16[512,1024]{1,0:T(8,128)(2,1)S(1)}, bf16[512,1024]{1,0:T(8,128)(2,1)}, u32[]{:S(2)}) copy-start(bf16[512,1024]{1,0:T(8,128)(2,1)} %reduce-scatter.5.cloned.1.call-done) | copy-start | bytes 3145732
  285.0 113.8 %all-gather.13.cloned.1.call-start = ((), (), s32[]{:S(2)}) async-start(), calls=%async_computation.10 | async-start | bytes 5242880 | tf_op jit(solution)/shard_map/all_gather | solution.py:187
  313.1 49.7 %copy-start.13 = (bf16[512,1024]{1,0:T(8,128)(2,1)S(1)}, bf16[512,1024]{1,0:T(8,128)(2,1)}, u32[]{:S(2)}) copy-start(bf16[512,1024]{1,0:T(8,128)(2,1)} %param.25) | copy-start | bytes 3145732
  364.1 265.1 %all-reduce.7.cloned.1.call-start = ((), (), s32[]{:S(2)}) async-start(), calls=%async_computation.13 | async-start | bytes 9437184 | tf_op jit(solution)/shard_map/psum | solution.py:216
  373.8 25.0 %copy-start.31 = (bf16[256,1024]{1,0:T(8,128)(2,1)S(1)}, bf16[256,1024]{1,0:T(8,128)(2,1)}, u32[]{:S(2)}) copy-start(bf16[256,1024]{1,0:T(8,128)(2,1)} %param.17) | copy-start | bytes 1572868
  423.9 23.3 %slice-start = ((s8[8388608]{0:T(1024)(128)(4,1)}), s8[4194304]{0:T(1024)(128)(4,1)S(1)}, s32[]{:S(2)}) async-start(s8[8388608]{0:T(1024)(128)(4,1)} %bitcast.124), calls=%async_computation.14 | async-start | bytes 8388608
  423.9 23.3 %slice-start.1 = ((s8[8388608]{0:T(1024)(128)(4,1)}), s8[4194304]{0:T(1024)(128)(4,1)S(1)}, s32[]{:S(2)}) async-start(s8[8388608]{0:T(1024)(128)(4,1)} %bitcast.124), calls=%async_computation.15 | async-start | bytes 8388608
  459.0 216.5 %reduce-scatter.11.cloned.1.call-start = ((), (), s32[]{:S(2)}) async-start(), calls=%async_computation.11 | async-start | bytes 5242880 | tf_op jit(solution)/shard_map/reduce_scatter | solution.py:208
  487.2 367.4 %all-gather.15.cloned.1.call-start = ((), (), s32[]{:S(2)}) async-start(), calls=%async_computation.12 | async-start | bytes 14155776 | tf_op jit(solution)/shard_map/all_gather | solution.py:10
  635.6 39.8 %copy-start.35 = (f32[1,1024]{1,0:T(1,128)S(1)}, f32[1,1024]{1,0:T(1,128)}, u32[]{:S(2)}) copy-start(f32[1,1024]{1,0:T(1,128)} %copy-done.34) | copy-start | bytes 12292
  635.6 39.8 %copy-start.37 = (f32[512]{0:T(512)S(1)}, f32[512]{0:T(512)}, u32[]{:S(2)}) copy-start(f32[512]{0:T(512)} %copy-done.36) | copy-start | bytes 6148
  635.6 41.7 %copy-start.43 = (f32[512]{0:T(512)S(1)}, f32[512]{0:T(512)}, u32[]{:S(2)}) copy-start(f32[512]{0:T(512)} %copy-done.42) | copy-start | bytes 6148
  635.6 41.7 %copy-start.41 = (f32[512]{0:T(512)S(1)}, f32[512]{0:T(512)}, u32[]{:S(2)}) copy-start(f32[512]{0:T(512)} %copy-done.40) | copy-start | bytes 6148
  635.6 88.5 %copy-start.10 = (f32[512,1024]{1,0:T(8,128)S(1)}, f32[512,1024]{1,0:T(8,128)}, u32[]{:S(2)}) copy-start(f32[512,1024]{1,0:T(8,128)} %copy-done.9) | copy-start | bytes 6291460
  (40 other events, 194.4 us)
Sparse Core Ops, SparseCore 0:
  15.5 37.1 all-gather.6
  110.2 44.5 reduce-scatter.4
  160.1 34.4 all-gather.8
  196.0 34.4 all-gather.10
  266.2 44.5 reduce-scatter.8
  313.2 44.5 reduce-scatter.6
  364.3 34.4 all-gather.12
  459.1 170.1 all-reduce.6
  631.8 43.5 reduce-scatter.10
  677.5 177.0 all-gather.14
